TPU v7x, 32 devices: a whole 2x2x4 slice. The times are simulated.
32 devices in a mesh: sys: 2 (over y), row: 2 (over x), col: 4 (over z), aux: 2 (over core).
Axes of the slice: x: 2, y: 2, z: 4, core: 2. Of those that a mesh axis runs over, the one named last changes fastest.
Arguments:
- coef_three: bfloat16 [4, 4, 512, 16384], P(('sys', 'row'), 'col', 'aux'), parts along dimension 0, may hold values from -6 to 6
- orbitals: bfloat16 [4, 4, 40, 128], P(('sys', 'row'), 'col'), parts along dimension 0, may hold values from -0.5 to 0.5
- density: bfloat16 [4, 4, 128, 128], P(('sys', 'row'), 'col'), parts along dimension 0, may hold values from -0.5 to 0.5
- pair_mask: int32 [4, 4, 8], P(('sys', 'row'), 'col'), parts along dimension 0, may hold values 0 or 1
Outputs:
- exch_self: float32 [4, 4, 128, 128], P(('sys', 'row'), 'col', 'aux'), parts along dimension 0
- exch_pair: float32 [4, 4, 8, 128, 128], P(('sys', 'row'), 'col', None, 'aux'), parts along dimension 0
- exch_full: float32 [4, 4, 128, 128], P(('sys', 'row'), 'col', 'aux'), parts along dimension 0
There are 2 independent parts, one for each index of `sys`. A program takes and returns all parts, laid end to end along the dimension named above; each array names one. Nothing has to cross between parts.
Inputs may be any that keep to these rules, and one draw needn't show every extreme that they name: `pair_mask`: entries for neighbours outside the grid are drawn like the others and have no effect.
All inputs are finite; a program needn't handle non-finite values. No bound on the sum of `pair_mask` on one device may be relied on, other than what follows from the above.
Results may differ from a plain program's by a relative error of at most 0.0041.
Values may be sent and summed in bfloat16 or wider, within the bound.
A program may use at most 192 MiB of HBM per device.

v0:
```python
import functools

import jax
import jax.numpy as jnp
from jax import lax
from jax.experimental import pallas as pl
from jax.experimental.pallas import tpu as pltpu
from jax.sharding import PartitionSpec as P

MESH = pl.DeviceIdType.MESH
LEFT, RIGHT, UP, DOWN, OWN = range(5)
OPPOSITE = (RIGHT, LEFT, DOWN, UP)
NAMES = (
    (OWN, LEFT), (OWN, RIGHT), (OWN, UP), (OWN, DOWN),
    (LEFT, UP), (LEFT, DOWN), (RIGHT, UP), (RIGHT, DOWN),
)
PLAN = (
    (((RIGHT, None), (UP, None), (DOWN, None)),
     ((OWN, LEFT), (OWN, DOWN), (LEFT, DOWN), (LEFT, UP))),
    (((LEFT, None), (UP, None), (DOWN, None)),
     ((OWN, RIGHT), (OWN, DOWN), (RIGHT, DOWN), (RIGHT, UP))),
    (((RIGHT, None), (LEFT, DOWN), (UP, None)),
     ((OWN, LEFT), (OWN, DOWN), (LEFT, DOWN), (RIGHT, DOWN))),
    (((RIGHT, UP), (LEFT, None), (DOWN, None)),
     ((OWN, RIGHT), (OWN, UP), (LEFT, UP), (RIGHT, UP))),
    (((RIGHT, DOWN), (LEFT, None), (UP, None)),
     ((OWN, RIGHT), (OWN, DOWN), (LEFT, DOWN), (RIGHT, DOWN))),
    (((RIGHT, None), (LEFT, UP), (DOWN, None)),
     ((OWN, LEFT), (OWN, UP), (LEFT, UP), (RIGHT, UP))),
)


def row_dot(left, right):
    return lax.dot_general(
        left, right, (((1,), (1,)), ((), ())), preferred_element_type=jnp.float32
    )


def cut(total):
    parts = len(PLAN)
    ends = [(total * i) // parts for i in range(parts + 1)]
    return list(zip(ends[:-1], ends[1:]))


def exchange_kernel(
    rows, cols, coef_hbm, orb_ref, dens_ref, out_ref,
    blocks, coef, stage, dens_half, acc, outbox, inbox, local, final, aux_local, aux_final,
    load_sem, send_sem, recv_sem, box_send, box_recv, aux_send, aux_recv,
):
    occ, basis = orb_ref.shape
    q_local = coef_hbm.shape[0]
    r, c, a = lax.axis_index("row"), lax.axis_index("col"), lax.axis_index("aux")
    has = (c > 0, c < cols - 1, r > 0, r < rows - 1)
    where = ({"col": c - 1}, {"col": c + 1}, {"row": r - 1}, {"row": r + 1})
    partner = {"aux": 1 - a}
    slices = cut(occ)

    parts, _, lanes = stage.shape
    block = stage.shape[1] // basis
    steps = basis // block

    def load(part, step):
        to = pl.multiple_of(step * (block * basis), block * basis)
        piece = (pl.ds(part * lanes, lanes), pl.ds(to, block * basis))
        return pltpu.make_async_copy(
            coef_hbm.at[piece], coef.at[piece], load_sem.at[part, step]
        )

    for part in range(parts):
        for step in range(steps):
            load(part, step).start()

    barrier = pltpu.get_barrier_semaphore()
    pl.semaphore_signal(barrier, inc=1, device_id=partner, device_id_type=MESH)
    for side in range(4):
        @pl.when(has[side])
        def _(side=side):
            pl.semaphore_signal(barrier, inc=1, device_id=where[side], device_id_type=MESH)
    expected = 1 + sum(flag.astype(jnp.int32) for flag in has)
    pl.semaphore_wait(barrier, expected)

    def copy(index, part, side, slot):
        start, end = slices[index]
        piece = (pl.ds(start, end - start), slice(None), pl.ds(part * lanes, lanes))
        return pltpu.make_async_remote_copy(
            src_ref=blocks.at[(OWN,) + piece],
            dst_ref=blocks.at[(slot,) + piece],
            send_sem=send_sem.at[side, index, part],
            recv_sem=recv_sem.at[slot, index, part],
            device_id=where[side],
            device_id_type=MESH,
        )

    def transfer(index, part, side):
        return copy(index, part, side, OPPOSITE[side])

    def arrival(index, part, side):
        return copy(index, part, side, side)

    def both(first, second):
        return first if second is None else jnp.logical_and(first, second)

    def flag_of(condition):
        return None if condition is None else has[condition]

    orb = orb_ref[...]
    for part in range(parts):
        @pl.loop(0, steps)
        def _(step, part=part):
            load(part, step).wait()
            for m in range(block):
                at = pl.multiple_of((step * block + m) * basis, basis)
                stage[part, m * occ:(m + 1) * occ, :] = row_dot(
                    orb, coef[part * lanes:(part + 1) * lanes, pl.ds(at, basis)]
                )
            first = pl.multiple_of(step * block, block)
            for o in range(occ):
                piece = stage[part, pl.ds(o, block, stride=occ), :]
                blocks[OWN, o, pl.ds(first, block), part * lanes:(part + 1) * lanes] = (
                    piece.astype(jnp.bfloat16)
                )

        for index, (sends, _) in enumerate(PLAN):
            for side, condition in sends:
                @pl.when(both(has[side], flag_of(condition)))
                def _(index=index, part=part, side=side):
                    transfer(index, part, side).start()

    for index in range(len(NAMES)):
        acc[index] = jnp.zeros((basis, basis), jnp.float32)
    for side in range(4):
        @pl.when(jnp.logical_not(has[side]))
        def _(side=side):
            inbox[side] = jnp.zeros(inbox.shape[1:], jnp.float32)

    def product(first, second, start, end):
        left = jnp.concatenate([blocks[first, o] for o in range(start, end)], axis=1)
        right = jnp.concatenate([blocks[second, o] for o in range(start, end)], axis=1)
        return row_dot(left, right)

    dens_turned = dens_ref[...].astype(jnp.float32).T.astype(jnp.bfloat16)

    @pl.loop(0, steps)
    def _(step):
        for m in range(block):
            at = pl.multiple_of((step * block + m) * basis, basis)
            value = row_dot(dens_turned, coef[:, pl.ds(at, basis)])
            for part in range(stage.shape[0]):
                stage[part, m * basis:(m + 1) * basis, :] = (
                    value[:, part * lanes:(part + 1) * lanes]
                )

        first = pl.multiple_of(step * block, block)

        @pl.loop(0, basis // 8)
        def _(group):
            for k in range(8):
                s = group * 8 + k
                for part in range(stage.shape[0]):
                    piece = stage[part, pl.ds(s, block, stride=basis), :]
                    dens_half[s, pl.ds(first, block), part * lanes:(part + 1) * lanes] = (
                        piece.astype(jnp.bfloat16)
                    )

    local[0] = jnp.zeros((basis, basis), jnp.float32)
    local[1] = jnp.zeros((basis, basis), jnp.float32)

    @pl.loop(0, basis // 8)
    def _(group):
        left = jnp.concatenate([dens_half[group * 8 + k] for k in range(8)], axis=1)
        right = jnp.concatenate(
            [
                coef[:, pl.ds(pl.multiple_of((group * 8 + k) * basis, basis), basis)]
                for k in range(8)
            ],
            axis=0,
        )
        local[1] += jnp.dot(left, right, preferred_element_type=jnp.float32)

    @pl.loop(0, occ // 8)
    def _(group):
        mine = jnp.concatenate([blocks[OWN, group * 8 + k] for k in range(8)], axis=1)
        local[0] += row_dot(mine, mine)

    rows_out = basis // 2
    theirs = pl.ds(pl.multiple_of((1 - a) * rows_out, rows_out), rows_out)
    ours = pl.ds(pl.multiple_of(a * rows_out, rows_out), rows_out)

    def to_partner(source, target, which):
        return pltpu.make_async_remote_copy(
            src_ref=source.at[:, theirs, :],
            dst_ref=target,
            send_sem=aux_send.at[which],
            recv_sem=aux_recv.at[which],
            device_id=partner,
            device_id_type=MESH,
        )

    swap_local = to_partner(local, aux_local, 0)
    swap_local.start()

    for index, (sends, products) in enumerate(PLAN):
        start, end = slices[index]
        for side, condition in sends:
            source = OPPOSITE[side]

            @pl.when(both(has[source], flag_of(condition)))
            def _(index=index, source=source):
                for part in range(parts):
                    arrival(index, part, source).wait_recv()

        for first, second in products:
            there = has[second] if first == OWN else jnp.logical_and(has[first], has[second])

            @pl.when(there)
            def _(first=first, second=second, start=start, end=end):
                acc[NAMES.index((first, second))] += product(first, second, start, end)

    def post(side):
        return pltpu.make_async_remote_copy(
            src_ref=outbox.at[side],
            dst_ref=inbox.at[OPPOSITE[side]],
            send_sem=box_send.at[side],
            recv_sem=box_recv.at[OPPOSITE[side]],
            device_id=where[side],
            device_id_type=MESH,
        )

    def collect(side):
        return pltpu.make_async_remote_copy(
            src_ref=outbox.at[side],
            dst_ref=inbox.at[side],
            send_sem=box_send.at[side],
            recv_sem=box_recv.at[side],
            device_id=where[side],
            device_id_type=MESH,
        )

    def value(first, second):
        return acc[NAMES.index((first, second))]

    outbox[LEFT, 0] = value(OWN, LEFT).T
    outbox[LEFT, 1] = value(LEFT, UP)
    outbox[LEFT, 2] = value(LEFT, DOWN)
    outbox[RIGHT, 0] = value(OWN, RIGHT).T
    outbox[RIGHT, 1] = value(RIGHT, UP)
    outbox[RIGHT, 2] = value(RIGHT, DOWN)
    outbox[UP, 0] = value(OWN, UP).T
    outbox[UP, 1] = value(LEFT, UP).T
    outbox[UP, 2] = value(RIGHT, UP).T
    outbox[DOWN, 0] = value(OWN, DOWN).T
    outbox[DOWN, 1] = value(LEFT, DOWN).T
    outbox[DOWN, 2] = value(RIGHT, DOWN).T
    for side in range(4):
        @pl.when(has[side])
        def _(side=side):
            post(side).start()
    for side in range(4):
        @pl.when(has[side])
        def _(side=side):
            collect(side).wait_recv()

    final[0] = inbox[LEFT, 1] + inbox[UP, 1]
    final[1] = value(OWN, UP) + inbox[UP, 0]
    final[2] = inbox[RIGHT, 1] + inbox[UP, 2]
    final[3] = value(OWN, LEFT) + inbox[LEFT, 0]
    final[4] = value(OWN, RIGHT) + inbox[RIGHT, 0]
    final[5] = inbox[LEFT, 2] + inbox[DOWN, 1]
    final[6] = value(OWN, DOWN) + inbox[DOWN, 0]
    final[7] = inbox[RIGHT, 2] + inbox[DOWN, 2]
    swap_final = to_partner(final, aux_final, 1)
    swap_final.start()

    swap_local.wait_recv()
    out_ref[8] = local[0, ours, :] + aux_local[0]
    out_ref[9] = local[1, ours, :] + aux_local[1]
    swap_final.wait_recv()
    for d in range(8):
        out_ref[d] = final[d, ours, :] + aux_final[d]

    swap_local.wait_send()
    swap_final.wait_send()
    for side in range(4):
        @pl.when(has[side])
        def _(side=side):
            post(side).wait_send()
    for index, (sends, _) in enumerate(PLAN):
        for side, condition in sends:
            @pl.when(both(has[side], flag_of(condition)))
            def _(index=index, side=side):
                for part in range(parts):
                    transfer(index, part, side).wait_send()


def finish_kernel(scales, sums_ref, mask_ref, self_ref, pair_ref, full_ref):
    self_scale, pair_scale, full_scale = scales
    for d in range(8):
        factor = mask_ref[d].astype(jnp.float32)
        pair_ref[0, 0, d] = sums_ref[d] * pair_scale * factor
    self_ref[0, 0] = sums_ref[8] * self_scale
    full_ref[0, 0] = sums_ref[9] * full_scale


def local_step(rows, cols, aux, coef_three, orbitals, density, pair_mask):
    q_local, width = coef_three.shape[2:]
    occ, basis = orbitals.shape[2:]
    coef = coef_three[0, 0]
    q_total = q_local * aux
    scales = (
        1.0 / (q_total * occ), 1.0 / (q_total * occ) ** 0.5, 1.0 / (q_total * basis) ** 0.5
    )
    rows_out = basis // aux
    lanes = 128
    f32 = jnp.float32
    dma = pltpu.SemaphoreType.DMA
    vmem = pl.BlockSpec(memory_space=pltpu.VMEM)
    sums = pl.pallas_call(
        functools.partial(exchange_kernel, rows, cols),
        out_shape=jax.ShapeDtypeStruct((10, rows_out, basis), f32),
        in_specs=[
            pl.BlockSpec(memory_space=pl.ANY),
            vmem,
            vmem,
        ],
        out_specs=vmem,
        scratch_shapes=[
            pltpu.VMEM((5, occ, basis, q_local), jnp.bfloat16),
            pltpu.VMEM((q_local, width), jnp.bfloat16),
            pltpu.VMEM((q_local // lanes, 16 * basis, lanes), f32),
            pltpu.VMEM((basis, basis, q_local), jnp.bfloat16),
            pltpu.VMEM((8, basis, basis), f32),
            pltpu.VMEM((4, 3, basis, basis), f32),
            pltpu.VMEM((4, 3, basis, basis), f32),
            pltpu.VMEM((2, basis, basis), f32),
            pltpu.VMEM((8, basis, basis), f32),
            pltpu.VMEM((2, rows_out, basis), f32),
            pltpu.VMEM((8, rows_out, basis), f32),
            dma((q_local // lanes, basis // 16)),
            dma((4, len(PLAN), q_local // lanes)),
            dma((4, len(PLAN), q_local // lanes)),
            dma((4,)),
            dma((4,)),
            dma((2,)),
            dma((2,)),
        ],
        compiler_params=pltpu.CompilerParams(
            collective_id=0, has_side_effects=True, vmem_limit_bytes=56 << 20
        ),
        name="exchange",
    )(coef, orbitals[0, 0], density[0, 0])
    return pl.pallas_call(
        functools.partial(finish_kernel, scales),
        out_shape=(
            jax.ShapeDtypeStruct((1, 1, rows_out, basis), f32),
            jax.ShapeDtypeStruct((1, 1, 8, rows_out, basis), f32),
            jax.ShapeDtypeStruct((1, 1, rows_out, basis), f32),
        ),
        in_specs=[vmem, pl.BlockSpec(memory_space=pltpu.SMEM)],
        out_specs=(vmem, vmem, vmem),
        name="finish",
    )(sums, pair_mask[0, 0])


def solution(mesh):
    in_specs = (
        P(("sys", "row"), "col", "aux", None),
        P(("sys", "row"), "col", None, None),
        P(("sys", "row"), "col", None, None),
        P(("sys", "row"), "col", None),
    )
    out_specs = (
        P(("sys", "row"), "col", "aux", None),
        P(("sys", "row"), "col", None, "aux", None),
        P(("sys", "row"), "col", "aux", None),
    )
    body = functools.partial(local_step, mesh.shape["row"], mesh.shape["col"], mesh.shape["aux"])
    return jax.shard_map(body, mesh=mesh, in_specs=in_specs, out_specs=out_specs, check_vma=False)
```

profile of v0, /device:TPU:1, one launch (start us, length us, event | category | flops | bytes accessed | tf_op | source)
XLA Modules:
  0.0 60.5 jit_solution(2158094739115236710)
XLA Ops:
  0.6 58.1 %exchange.1.sums_ref = f32[10,64,128]{2,1,0:T(8,128)} custom-call(bf16[256,16384]{1,0:T(8,128)(2,1)} %bitcast.4, bf16[40,128]{1,0:T(8,128)(2,1)} %bitcast.6, bf16[128,128]{1,0:T(8,128)(2,1)} %bitcast.5), custom_call_target="tpu_custom_call" | custom-call | tf_op jit(solution)/shard_map/exchange/pallas_call | solution.py:317
  58.8 1.7 %finish.1 = (f32[1,1,64,128]{3,2,1,0:T(8,128)}, f32[1,1,8,64,128]{4,3,2,1,0:T(8,128)}, f32[1,1,64,128]{3,2,1,0:T(8,128)}) custom-call(f32[10,64,128]{2,1,0:T(8,128)} %exchange.1.sums_ref, s32[8]{0:T(128)} %bitcast.7), custom_call_target="tpu_custom_call" | custom-call | tf_op jit(solution)/shard_map/finish/pallas_call | solution.py:351
where the time goes:
time: 60.8 us; the launch traced here: 60.5 us
  Pallas kernels  59.8 us (98%)
  between operations  0.64 us (1%)
    pallas_call x1, Pallas kernels, local_step(): pl.pallas_call(functools.partial(exchange_kernel, rows, cols), out_shape=...  58.1 us
    pallas_call x1, Pallas kernels, local_step(): pl.pallas_call(functools.partial(finish_kernel, scales), out_shape=(jax.S...  1.72 us

commit v1 on v0

v1 whole, which is shorter than its diff:
```python
import functools

import jax
import jax.numpy as jnp
from jax import lax
from jax.experimental import pallas as pl
from jax.experimental.pallas import tpu as pltpu
from jax.sharding import PartitionSpec as P

MESH = pl.DeviceIdType.MESH
OWN, VERT, SIDE, SIDEV = range(4)
ROLES = ((0, 0), (0, 1), (1, 0), (1, 1))
BLOCK = 16
LAG = 6
WIRE = jnp.float32


def row_dot(left, right):
    return lax.dot_general(
        left, right, (((1,), (1,)), ((), ())), preferred_element_type=jnp.float32
    )


def odd_tiles(rows):
    tiles = -(-rows // 8)
    return 8 * (tiles + 1 - tiles % 2)


def chunk_of(occ):
    quarter = occ // 4
    return quarter, 2 if quarter % 2 == 0 else 1


def exchange_kernel(
    rows, cols, coef_hbm, orb_ref, dens_ref, out_ref,
    blocks, coef, stage, dens_half, acc, gram, local, outbox, outbox_v, inbox, inbox_v,
    aux_acc, aux_gram, aux_local,
    load_sem, vert_send, vert_recv, side_send, side_recv, pass_send, pass_recv,
    box_send, box_recv, boxv_send, boxv_recv, aux_send, aux_recv,
):
    occ, basis = orb_ref.shape
    r, c, a = lax.axis_index("row"), lax.axis_index("col"), lax.axis_index("aux")
    partner = {"aux": 1 - a}
    left, right, above, below = c > 0, c < cols - 1, r > 0, r < rows - 1
    both = jnp.logical_and
    parts, lanes = blocks.shape[1], blocks.shape[4]
    steps = basis // BLOCK
    quarter, size = chunk_of(occ)
    count = parts * 2 * (quarter // size)

    active = (below, above)
    vert_to = ({"row": r - 1}, {"row": r + 1})
    vert_from = ({"row": r + 1}, {"row": r - 1})
    first_v = jnp.where(below, 0, 1)
    end_v = jnp.where(above, 2, 1)

    def load(part, step):
        to = pl.multiple_of(step * (BLOCK * basis), BLOCK * basis)
        piece = (pl.ds(part * lanes, lanes), pl.ds(to, BLOCK * basis))
        return pltpu.make_async_copy(
            coef_hbm.at[piece], coef.at[piece], load_sem.at[part, step]
        )

    for part in range(parts):
        for step in range(steps):
            load(part, step).start()

    barrier = pltpu.get_barrier_semaphore()
    pl.semaphore_signal(barrier, inc=1, device_id=partner, device_id_type=MESH)
    expected = 1
    for dr, row_there in ((-1, above), (0, None), (1, below)):
        for dc, col_there in ((-1, left), (0, None), (1, right)):
            if dr == 0 and dc == 0:
                continue
            there = both(
                True if row_there is None else row_there,
                True if col_there is None else col_there,
            )
            expected = expected + there.astype(jnp.int32)

            @pl.when(there)
            def _(dr=dr, dc=dc):
                pl.semaphore_signal(
                    barrier, inc=1, device_id={"row": r + dr, "col": c + dc}, device_id_type=MESH
                )

    def place(v, j):
        per_part = count // parts
        part, rest = j // per_part, j % per_part
        h, sub = rest % 2, rest // 2
        return part, h, v * (2 * quarter) + h * quarter + sub * size

    def side_of(h):
        return {"col": c + 1 - 2 * h}

    def sends_side(h):
        return both(c + 1 - 2 * h >= 0, c + 1 - 2 * h < cols)

    def gets_side(h):
        return both(c - 1 + 2 * h >= 0, c - 1 + 2 * h < cols)

    def copy(v, j, source, target, send, recv, device):
        part, _, o = place(v, j)
        return pltpu.make_async_remote_copy(
            src_ref=blocks.at[source, part, pl.ds(o, size)],
            dst_ref=blocks.at[target, part, pl.ds(o, size)],
            send_sem=send.at[v, j],
            recv_sem=recv.at[v, j],
            device_id=device,
            device_id_type=MESH,
        )

    def vertical(v, j):
        return copy(v, j, OWN, VERT, vert_send, vert_recv, {"row": r - 1 + 2 * v})

    def sideways(v, j):
        return copy(v, j, OWN, SIDE, side_send, side_recv, side_of(place(v, j)[1]))

    def passed(v, j):
        return copy(v, j, VERT, SIDEV, pass_send, pass_recv, side_of(place(v, j)[1]))

    def each_active(body):
        @pl.loop(first_v, end_v)
        def _(v):
            body(v)

    orb = orb_ref[...]
    zero = jnp.zeros_like(orb)
    two = jnp.concatenate(
        [jnp.concatenate([orb, zero], axis=1), jnp.concatenate([zero, orb], axis=1)], axis=0
    )
    pitch = odd_tiles(occ)
    for part in range(parts):
        @pl.loop(0, steps)
        def _(step, part=part):
            load(part, step).wait()
            for m in range(0, BLOCK, 2):
                at = pl.multiple_of((step * BLOCK + m) * basis, 2 * basis)
                value = row_dot(
                    two, coef[part * lanes:(part + 1) * lanes, pl.ds(at, 2 * basis)]
                )
                for k in range(2):
                    to = (m + k) * pitch
                    stage[part, to:to + occ, :] = value[k * occ:(k + 1) * occ]
            first = pl.multiple_of(step * BLOCK, BLOCK)
            for o in range(occ):
                piece = stage[part, pl.ds(o, BLOCK, stride=pitch), :]
                blocks[OWN, part, o, pl.ds(first, BLOCK), :] = piece.astype(jnp.bfloat16)

        if part == 0:
            pl.semaphore_wait(barrier, expected)
        span = count // parts
        for v in range(2):
            @pl.when((above, below)[v])
            def _(v=v, part=part):
                @pl.loop(part * span, (part + 1) * span)
                def _(j):
                    vertical(v, j).start()

        @pl.loop(part * span, (part + 1) * span)
        def _(j):
            @pl.when(sends_side(place(0, j)[1]))
            def _():
                each_active(lambda v: sideways(v, j).start())

    def forward(j):
        def one(v):
            vertical(v, j).wait_recv()

            @pl.when(sends_side(place(v, j)[1]))
            def _():
                passed(v, j).start()

        each_active(one)

    acc[...] = jnp.zeros(acc.shape, jnp.float32)
    gram[...] = jnp.zeros(gram.shape, jnp.float32)
    local[...] = jnp.zeros(local.shape, jnp.float32)

    dens_turned = dens_ref[...].astype(jnp.float32).T.astype(jnp.bfloat16)
    wide = odd_tiles(basis)
    early = steps // 2

    @pl.loop(0, steps)
    def _(step):
        for m in range(BLOCK):
            at = pl.multiple_of((step * BLOCK + m) * basis, basis)
            value = row_dot(dens_turned, coef[:, pl.ds(at, basis)])
            for part in range(parts):
                stage[part, m * wide:m * wide + basis, :] = (
                    value[:, part * lanes:(part + 1) * lanes]
                )
        first = pl.multiple_of(step * BLOCK, BLOCK)
        for s in range(basis):
            for part in range(parts):
                piece = stage[part, pl.ds(s, BLOCK, stride=wide), :]
                dens_half[s, pl.ds(first, BLOCK), part * lanes:(part + 1) * lanes] = (
                    piece.astype(jnp.bfloat16)
                )

        @pl.when(step % 2 == 1)
        def _():
            forward(step // 2)

    groups = basis // 8

    @pl.loop(0, groups)
    def _(group):
        left_side = jnp.concatenate([dens_half[group * 8 + k] for k in range(8)], axis=1)
        right_side = jnp.concatenate(
            [
                coef[:, pl.ds(pl.multiple_of((group * 8 + k) * basis, basis), basis)]
                for k in range(8)
            ],
            axis=0,
        )
        local[1] += jnp.dot(left_side, right_side, preferred_element_type=jnp.float32)

        @pl.when(group % 4 == 3)
        def _():
            forward(early + group // 4)

    forwarded = early + groups // 4

    for v in range(2):
        @pl.when(jnp.logical_not(active[v]))
        def _(v=v):
            @pl.loop(0, count)
            def _(j):
                part, _, o = place(v, j)
                mine = jnp.concatenate([blocks[OWN, part, o + k] for k in range(size)], axis=1)
                local[0] += row_dot(mine, mine)

    def products(j):
        def one(v):
            part, h, o = place(v, j)

            def wide_rows(first_slot):
                return jnp.concatenate(
                    [
                        jnp.concatenate([blocks[slot, part, o + k] for k in range(size)], axis=1)
                        for slot in (first_slot, first_slot + 1)
                    ],
                    axis=0,
                )

            here = wide_rows(OWN)
            gram[v] += row_dot(here, here)

            @pl.when(gets_side(h))
            def _():
                sideways(v, j).wait_recv()
                passed(v, j).wait_recv()
                near, there = wide_rows(OWN), wide_rows(SIDE)
                acc[v, h, 0] += row_dot(near, there)
                acc[v, h, 1] += row_dot(there, near)

        each_active(one)

    @pl.loop(0, forwarded - LAG)
    def _(j):
        products(j)

    @pl.loop(forwarded, count)
    def _(j):
        forward(j)
        products(j - LAG)

    @pl.loop(count - LAG, count)
    def _(j):
        products(j)

    rows_out = basis // 2
    theirs = pl.multiple_of((1 - a) * rows_out, rows_out)
    ours = pl.multiple_of(a * rows_out, rows_out)

    def to_partner(source, target, which):
        return pltpu.make_async_remote_copy(
            src_ref=source,
            dst_ref=target,
            send_sem=aux_send.at[which],
            recv_sem=aux_recv.at[which],
            device_id=partner,
            device_id_type=MESH,
        )

    def swap_acc(v, h, side, half):
        return to_partner(
            acc.at[v, h, side, pl.ds(half * basis + theirs, rows_out)],
            aux_acc.at[v, h, side, half],
            8 * v + 4 * h + 2 * side + half,
        )

    def swap_gram(v, half):
        return to_partner(
            gram.at[v, pl.ds(half * basis + theirs, rows_out)],
            aux_gram.at[v, half],
            16 + 2 * v + half,
        )

    swap_local = to_partner(local.at[:, pl.ds(theirs, rows_out)], aux_local, 20)
    halves = ((0, 1), (1, 0), (1, 1), (0, 0))
    has = [both(active[v], gets_side(h)) for v, h in ROLES]

    for index, (v, h) in enumerate(ROLES):
        @pl.when(has[index])
        def _(v=v, h=h):
            for side, half in halves:
                swap_acc(v, h, side, half).start()
    for v in range(2):
        @pl.when(active[v])
        def _(v=v):
            for half in range(2):
                swap_gram(v, half).start()
    swap_local.start()

    def box(v, h, kind):
        row, col = r + 1 - 2 * v, c - 1 + 2 * h
        device = ({"row": row}, {"col": col}, {"row": row, "col": col})[kind]
        return pltpu.make_async_remote_copy(
            src_ref=outbox.at[v, h, kind],
            dst_ref=inbox.at[v, h, kind],
            send_sem=box_send.at[v, h, kind],
            recv_sem=box_recv.at[v, h, kind],
            device_id=device,
            device_id_type=MESH,
        )

    def box_v(v):
        return pltpu.make_async_remote_copy(
            src_ref=outbox_v.at[v],
            dst_ref=inbox_v.at[v],
            send_sem=boxv_send.at[v],
            recv_sem=boxv_recv.at[v],
            device_id=vert_from[v],
            device_id_type=MESH,
        )

    up_down = (above, below)
    arrives = [
        (
            both(up_down[v], (left, right)[h]),
            both(active[v], (right, left)[h]),
            both(up_down[v], (right, left)[h]),
        )
        for v, h in ROLES
    ]
    for index, (v, h) in enumerate(ROLES):
        for kind in range(3):
            @pl.when(jnp.logical_not(arrives[index][kind]))
            def _(v=v, h=h, kind=kind):
                inbox[v, h, kind] = jnp.zeros(inbox.shape[3:], inbox.dtype)

        @pl.when(jnp.logical_not(has[index]))
        def _(v=v, h=h):
            acc[v, h, 0, pl.ds(ours, rows_out), :] = jnp.zeros(
                (rows_out, 2 * basis), jnp.float32
            )
            aux_acc[v, h, 0, 0] = jnp.zeros((rows_out, 2 * basis), jnp.float32)
    for v in range(2):
        @pl.when(jnp.logical_not(up_down[v]))
        def _(v=v):
            inbox_v[v] = jnp.zeros(inbox_v.shape[1:], inbox_v.dtype)

        @pl.when(jnp.logical_not(active[v]))
        def _(v=v):
            aux_gram[v, 0] = jnp.zeros((rows_out, 2 * basis), jnp.float32)

    for index, (v, h) in enumerate(ROLES):
        @pl.when(has[index])
        def _(v=v, h=h):
            for side, half in halves[:3]:
                swap_acc(v, h, side, half).wait_recv()
                kind = 2 * side + half - 1
                outbox[v, h, kind] = (
                    acc[v, h, side, pl.ds(half * basis + ours, rows_out), :]
                    + aux_acc[v, h, side, half]
                ).astype(outbox.dtype)
                box(v, h, kind).start()
    for v in range(2):
        @pl.when(active[v])
        def _(v=v):
            swap_gram(v, 1).wait_recv()
            outbox_v[v] = (
                gram[v, pl.ds(basis + ours, rows_out), :basis] + aux_gram[v, 1, :, :basis]
            ).astype(outbox_v.dtype)
            box_v(v).start()

    total = [None] * 8

    def add(d, value):
        total[d] = value if total[d] is None else total[d] + value

    swap_local.wait_recv()
    own = local[0, pl.ds(ours, rows_out), :] + aux_local[0]
    out_ref[9] = local[1, pl.ds(ours, rows_out), :] + aux_local[1]
    for v in range(2):
        @pl.when(active[v])
        def _(v=v):
            swap_gram(v, 0).wait_recv()

        value = gram[v, pl.ds(ours, rows_out), :] + aux_gram[v, 0]
        own = own + value[:, :basis]
        add((6, 1)[v], value[:, basis:])
    out_ref[8] = own

    far = ((5, 7), (0, 2))
    for index, (v, h) in enumerate(ROLES):
        @pl.when(has[index])
        def _(v=v, h=h):
            swap_acc(v, h, 0, 0).wait_recv()

        value = acc[v, h, 0, pl.ds(ours, rows_out), :] + aux_acc[v, h, 0, 0]
        add((3, 4)[h], value[:, :basis])
        add(far[v][h], value[:, basis:])

    for v in range(2):
        @pl.when(up_down[v])
        def _(v=v):
            box_v(v).wait_recv()

        add((1, 6)[v], inbox_v[v].astype(jnp.float32))

    last = (jnp.logical_not(below), jnp.logical_not(above))
    for index, (v, h) in enumerate(ROLES):
        for kind in range(3):
            @pl.when(arrives[index][kind])
            def _(v=v, h=h, kind=kind):
                box(v, h, kind).wait_recv()

        vert, side, diag = (inbox[v, h, kind].astype(jnp.float32) for kind in range(3))
        edge = last[v].astype(jnp.float32)
        add(far[1 - v][h], vert[:, :basis])
        add((3, 4)[h], vert[:, basis:] * edge)
        add((4, 3)[h], side[:, :basis])
        add(far[v][1 - h], side[:, basis:])
        add(far[1 - v][1 - h], diag[:, :basis])
        add((4, 3)[h], diag[:, basis:] * edge)
    for d in range(8):
        out_ref[d] = total[d]

    for v in range(2):
        @pl.when(up_down[v])
        def _(v=v):
            @pl.loop(0, count)
            def _(j):
                vertical(v, j).wait_send()

    @pl.loop(0, count)
    def _(j):
        @pl.when(sends_side(place(0, j)[1]))
        def _():
            def one(v):
                sideways(v, j).wait_send()
                passed(v, j).wait_send()

            each_active(one)

    for index, (v, h) in enumerate(ROLES):
        @pl.when(has[index])
        def _(v=v, h=h):
            for side, half in halves:
                swap_acc(v, h, side, half).wait_send()
            for kind in range(3):
                box(v, h, kind).wait_send()
    for v in range(2):
        @pl.when(active[v])
        def _(v=v):
            for half in range(2):
                swap_gram(v, half).wait_send()
            box_v(v).wait_send()
    swap_local.wait_send()


def finish_kernel(scales, sums_ref, mask_ref, self_ref, pair_ref, full_ref):
    self_scale, pair_scale, full_scale = scales
    for d in range(8):
        factor = mask_ref[d].astype(jnp.float32)
        pair_ref[0, 0, d] = sums_ref[d] * pair_scale * factor
    self_ref[0, 0] = sums_ref[8] * self_scale
    full_ref[0, 0] = sums_ref[9] * full_scale


def local_step(rows, cols, aux, coef_three, orbitals, density, pair_mask):
    q_local, width = coef_three.shape[2:]
    occ, basis = orbitals.shape[2:]
    coef = coef_three[0, 0]
    q_total = q_local * aux
    scales = (
        1.0 / (q_total * occ), 1.0 / (q_total * occ) ** 0.5, 1.0 / (q_total * basis) ** 0.5
    )
    rows_out = basis // aux
    lanes = 128
    parts = q_local // lanes
    quarter, size = chunk_of(occ)
    count = parts * 2 * (quarter // size)
    f32, bf16 = jnp.float32, jnp.bfloat16
    dma = pltpu.SemaphoreType.DMA
    vmem = pl.BlockSpec(memory_space=pltpu.VMEM)
    sums = pl.pallas_call(
        functools.partial(exchange_kernel, rows, cols),
        out_shape=jax.ShapeDtypeStruct((10, rows_out, basis), f32),
        in_specs=[
            pl.BlockSpec(memory_space=pl.ANY),
            vmem,
            vmem,
        ],
        out_specs=vmem,
        scratch_shapes=[
            pltpu.VMEM((4, parts, occ, basis, lanes), bf16),
            pltpu.VMEM((q_local, width), bf16),
            pltpu.VMEM((parts, BLOCK * max(odd_tiles(basis), odd_tiles(occ)), lanes), f32),
            pltpu.VMEM((basis, basis, q_local), bf16),
            pltpu.VMEM((2, 2, 2, 2 * basis, 2 * basis), f32),
            pltpu.VMEM((2, 2 * basis, 2 * basis), f32),
            pltpu.VMEM((2, basis, basis), f32),
            pltpu.VMEM((2, 2, 3, rows_out, 2 * basis), WIRE),
            pltpu.VMEM((2, rows_out, basis), WIRE),
            pltpu.VMEM((2, 2, 3, rows_out, 2 * basis), WIRE),
            pltpu.VMEM((2, rows_out, basis), WIRE),
            pltpu.VMEM((2, 2, 2, 2, rows_out, 2 * basis), f32),
            pltpu.VMEM((2, 2, rows_out, 2 * basis), f32),
            pltpu.VMEM((2, rows_out, basis), f32),
            dma((parts, basis // BLOCK)),
            dma((2, count)),
            dma((2, count)),
            dma((2, count)),
            dma((2, count)),
            dma((2, count)),
            dma((2, count)),
            dma((2, 2, 3)),
            dma((2, 2, 3)),
            dma((2,)),
            dma((2,)),
            dma((21,)),
            dma((21,)),
        ],
        compiler_params=pltpu.CompilerParams(
            collective_id=0, has_side_effects=True, vmem_limit_bytes=56 << 20
        ),
        name="exchange",
    )(coef, orbitals[0, 0], density[0, 0])
    return pl.pallas_call(
        functools.partial(finish_kernel, scales),
        out_shape=(
            jax.ShapeDtypeStruct((1, 1, rows_out, basis), f32),
            jax.ShapeDtypeStruct((1, 1, 8, rows_out, basis), f32),
            jax.ShapeDtypeStruct((1, 1, rows_out, basis), f32),
        ),
        in_specs=[vmem, pl.BlockSpec(memory_space=pltpu.SMEM)],
        out_specs=(vmem, vmem, vmem),
        name="finish",
    )(sums, pair_mask[0, 0])


def solution(mesh):
    in_specs = (
        P(("sys", "row"), "col", "aux", None),
        P(("sys", "row"), "col", None, None),
        P(("sys", "row"), "col", None, None),
        P(("sys", "row"), "col", None),
    )
    out_specs = (
        P(("sys", "row"), "col", "aux", None),
        P(("sys", "row"), "col", None, "aux", None),
        P(("sys", "row"), "col", "aux", None),
    )
    body = functools.partial(local_step, mesh.shape["row"], mesh.shape["col"], mesh.shape["aux"])
    return jax.shard_map(body, mesh=mesh, in_specs=in_specs, out_specs=out_specs, check_vma=False)
```

time: 60.8 us -> 54.7 us (0.90)
  the two profiles are of different devices: /device:TPU:1 before, /device:TPU:17 now
where the time goes in v1:
time: 54.7 us; the launch traced here: 54.5 us
  Pallas kernels  53.9 us (99%)
  between operations  0.64 us (1%)
    pallas_call x1, Pallas kernels, local_step(): pl.pallas_call(functools.partial(exchange_kernel, rows, cols), out_shape=...  52.2 us
    pallas_call x1, Pallas kernels, local_step(): pl.pallas_call(functools.partial(finish_kernel, scales), out_shape=(jax.S...  1.72 us

profile of v1, /device:TPU:17, one launch (start us, length us, event | category | flops | bytes accessed | tf_op | source)
XLA Modules:
  0.0 54.5 jit_solution(13023479425259120878)
XLA Ops:
  0.6 52.2 %exchange.1.sums_ref = f32[10,64,128]{2,1,0:T(8,128)} custom-call(bf16[256,16384]{1,0:T(8,128)(2,1)} %bitcast.4, bf16[40,128]{1,0:T(8,128)(2,1)} %bitcast.6, bf16[128,128]{1,0:T(8,128)(2,1)} %bitcast.5), custom_call_target="tpu_custom_call" | custom-call | tf_op jit(solution)/shard_map/exchange/pallas_call | solution.py:500
  52.8 1.7 %finish.1 = (f32[1,1,64,128]{3,2,1,0:T(8,128)}, f32[1,1,8,64,128]{4,3,2,1,0:T(8,128)}, f32[1,1,64,128]{3,2,1,0:T(8,128)}) custom-call(f32[10,64,128]{2,1,0:T(8,128)} %exchange.1.sums_ref, s32[8]{0:T(128)} %bitcast.7), custom_call_target="tpu_custom_call" | custom-call | tf_op jit(solution)/shard_map/finish/pallas_call | solution.py:543

commit v2 on v1

v2 whole, which is shorter than its diff:
```python
import functools

import jax
import jax.numpy as jnp
from jax import lax
from jax.experimental import pallas as pl
from jax.experimental.pallas import tpu as pltpu
from jax.sharding import PartitionSpec as P

MESH = pl.DeviceIdType.MESH
OWN, VERT, SIDE, SIDEV = range(4)
ROLES = ((0, 0), (0, 1), (1, 0), (1, 1))
BLOCK = 16
CUTS = 4
LAG = 3
WIRE = jnp.bfloat16


def row_dot(left, right):
    return lax.dot_general(
        left, right, (((1,), (1,)), ((), ())), preferred_element_type=jnp.float32
    )


def odd_tiles(rows):
    tiles = -(-rows // 8)
    return 8 * (tiles + 1 - tiles % 2)


def chunks_of(occ):
    quarter = occ // 4
    size = 2 if quarter % 2 == 0 else 1
    return quarter, size, quarter // size


def exchange_kernel(
    rows, cols, coef_hbm, orb_hbm, dens_hbm, out_ref,
    blocks, coef, orb_ref, dens_ref, stage, dens_half, acc, gram, local,
    outbox, outbox_v, inbox, inbox_v, aux_acc, aux_gram, aux_local,
    load_sem, small_sem, vert_send, vert_recv, side_send, side_recv, pass_send, pass_recv,
    box_send, box_recv, boxv_send, boxv_recv, aux_send, aux_recv,
):
    occ, basis = orb_ref.shape
    r, c, a = lax.axis_index("row"), lax.axis_index("col"), lax.axis_index("aux")
    partner = {"aux": 1 - a}
    left, right, above, below = c > 0, c < cols - 1, r > 0, r < rows - 1
    both = jnp.logical_and
    parts, lanes = blocks.shape[1], blocks.shape[4]
    steps = basis // BLOCK
    width = coef.shape[1]
    quarter, size, subs = chunks_of(occ)
    numbers = ((parts - 1) * subs, parts * subs)

    active = (below, above)
    up_down = (above, below)
    vert_from = ({"row": r + 1}, {"row": r - 1})
    first_v = jnp.where(below, 0, 1)
    end_v = jnp.where(above, 2, 1)

    span = width // CUTS

    def load(part, k):
        piece = (pl.ds(part * lanes, lanes), pl.ds(pl.multiple_of(k * span, span), span))
        return pltpu.make_async_copy(
            coef_hbm.at[piece], coef.at[piece], load_sem.at[part, k]
        )

    load_orb = pltpu.make_async_copy(orb_hbm, orb_ref, small_sem.at[0])
    load_dens = pltpu.make_async_copy(dens_hbm, dens_ref, small_sem.at[1])
    load_orb.start()
    load(0, 0).start()

    barrier = pltpu.get_barrier_semaphore()
    pl.semaphore_signal(barrier, inc=1, device_id=partner, device_id_type=MESH)
    expected = 1
    for dr, row_there in ((-1, above), (0, None), (1, below)):
        for dc, col_there in ((-1, left), (0, None), (1, right)):
            if dr == 0 and dc == 0:
                continue
            there = both(
                True if row_there is None else row_there,
                True if col_there is None else col_there,
            )
            expected = expected + there.astype(jnp.int32)

            @pl.when(there)
            def _(dr=dr, dc=dc):
                pl.semaphore_signal(
                    barrier, inc=1, device_id={"row": r + dr, "col": c + dc}, device_id_type=MESH
                )

    def side_of(h):
        return {"col": c + 1 - 2 * h}

    def sends_side(h):
        return both(c + 1 - 2 * h >= 0, c + 1 - 2 * h < cols)

    def gets_side(h):
        return both(c - 1 + 2 * h >= 0, c - 1 + 2 * h < cols)

    def slot(v):
        return v if rows > 2 else 0

    def copy(source, target, piece, send, recv, device):
        return pltpu.make_async_remote_copy(
            src_ref=blocks.at[(source,) + piece],
            dst_ref=blocks.at[(target,) + piece],
            send_sem=send,
            recv_sem=recv,
            device_id=device,
            device_id_type=MESH,
        )

    cut = basis // CUTS

    def start_of(v, h):
        return v * (2 * quarter) + h * quarter

    def row_of(v):
        return {"row": r - 1 + 2 * v}

    def sideways(v, h, piece):
        pair = (slot(v), h)
        return copy(OWN, SIDE, piece, side_send.at[pair], side_recv.at[pair], side_of(h))

    def sideways_cut(v, h, k):
        return sideways(v, h, (0, pl.ds(start_of(v, h), quarter), pl.ds(k * cut, cut)))

    def sideways_part(v, h, part):
        return sideways(v, h, (part, pl.ds(start_of(v, h), quarter)))

    def sideways_all(v, h):
        return sideways(v, h, (slice(None), pl.ds(start_of(v, h), quarter)))

    def up_or_down(v, piece, k):
        send, recv = vert_send.at[slot(v)], vert_recv.at[slot(v), k]
        return copy(OWN, VERT, piece, send, recv, row_of(v))

    def vertical_cut(v, k):
        return up_or_down(v, (0, pl.ds(start_of(v, 0), quarter), pl.ds(k * cut, cut)), 0)

    def vertical_first(v):
        return up_or_down(v, (0, pl.ds(start_of(v, 0), quarter)), 0)

    def vertical_all(v):
        return up_or_down(v, (slice(None), pl.ds(start_of(v, 0), 2 * quarter)), 0)

    def place(h, n):
        return 1 - h + n // subs, (n % subs) * size

    def chunk(v, h, n):
        part, o = place(h, n)
        return part, pl.ds(start_of(v, h) + o, size)

    def vertical(v, h, n):
        return up_or_down(v, chunk(v, h, n), 1 + h * numbers[0] + n)

    def pass_piece(v, h, piece, k):
        send, recv = pass_send.at[slot(v), h], pass_recv.at[slot(v), k]
        return copy(VERT, SIDEV, piece, send, recv, side_of(h))

    def passed_first(v):
        return pass_piece(v, 0, (0, pl.ds(start_of(v, 0), quarter)), 0)

    def passed(v, h, n):
        return pass_piece(v, h, chunk(v, h, n), 1 + h * numbers[0] + n)

    def passed_all(v, h):
        return pass_piece(v, h, (slice(None), pl.ds(start_of(v, h), quarter)), 0)

    def each_active(body):
        @pl.loop(first_v, end_v)
        def _(v):
            body(v)

    load_orb.wait()
    for part in range(parts):
        for k in range(CUTS):
            if part + k > 0:
                load(part, k).start()
    load_dens.start()
    orb = orb_ref[...]
    zero = jnp.zeros_like(orb)
    two = jnp.concatenate(
        [jnp.concatenate([orb, zero], axis=1), jnp.concatenate([zero, orb], axis=1)], axis=0
    )
    pitch = odd_tiles(occ)

    def half_transform(part, first_step, end_step):
        @pl.loop(first_step, end_step)
        def _(step):
            @pl.when(step % (steps // CUTS) == 0)
            def _():
                load(part, step // (steps // CUTS)).wait()

            for m in range(0, BLOCK, 2):
                at = pl.multiple_of((step * BLOCK + m) * basis, 2 * basis)
                value = row_dot(
                    two, coef[part * lanes:(part + 1) * lanes, pl.ds(at, 2 * basis)]
                )
                for k in range(2):
                    to = (m + k) * pitch
                    stage[part, to:to + occ, :] = value[k * occ:(k + 1) * occ]
            first = pl.multiple_of(step * BLOCK, BLOCK)
            for o in range(occ):
                piece = stage[part, pl.ds(o, BLOCK, stride=pitch), :]
                blocks[OWN, part, o, pl.ds(first, BLOCK), :] = piece.astype(jnp.bfloat16)

    for k in range(CUTS):
        half_transform(0, k * steps // CUTS, (k + 1) * steps // CUTS)
        if k == 0:
            pl.semaphore_wait(barrier, expected)
        for v in range(2):
            @pl.when(up_down[v])
            def _(v=v, k=k):
                vertical_cut(v, k).start()
        for v, h in ROLES:
            @pl.when(both(active[v], sends_side(h)))
            def _(v=v, h=h, k=k):
                sideways_cut(v, h, k).start()

    def start_vertical(h, first, end):
        for v in range(2):
            @pl.when(up_down[v])
            def _(v=v):
                @pl.loop(first, end)
                def _(n):
                    vertical(v, h, n).start()

    start_vertical(1, 0, subs)
    for part in range(1, parts):
        half_transform(part, 0, steps)
        start_vertical(0, (part - 1) * subs, part * subs)
        start_vertical(1, part * subs, (part + 1) * subs)
        for v, h in ROLES:
            @pl.when(both(active[v], sends_side(h)))
            def _(v=v, h=h, part=part):
                sideways_part(v, h, part).start()
    local[...] = jnp.zeros(local.shape, jnp.float32)
    load_dens.wait()
    dens_turned = dens_ref[...].astype(jnp.float32).T.astype(jnp.bfloat16)
    wide = odd_tiles(basis)

    @pl.loop(0, steps)
    def _(step):
        for m in range(BLOCK):
            at = pl.multiple_of((step * BLOCK + m) * basis, basis)
            value = row_dot(dens_turned, coef[:, pl.ds(at, basis)])
            for part in range(parts):
                stage[part, m * wide:m * wide + basis, :] = (
                    value[:, part * lanes:(part + 1) * lanes]
                )
        first = pl.multiple_of(step * BLOCK, BLOCK)
        for s in range(basis):
            for part in range(parts):
                piece = stage[part, pl.ds(s, BLOCK, stride=wide), :]
                dens_half[s, pl.ds(first, BLOCK), part * lanes:(part + 1) * lanes] = (
                    piece.astype(jnp.bfloat16)
                )

    def orbitals_of(slots, part, o, number):
        return jnp.concatenate(
            [
                jnp.concatenate([blocks[slot, part, o + k] for k in range(number)], axis=1)
                for slot in slots
            ],
            axis=0,
        )

    def pass_first(v):
        vertical_first(v).wait_recv()

        @pl.when(sends_side(0))
        def _():
            passed_first(v).start()

    def pass_on(h, n):
        def one(v):
            vertical(v, h, n).wait_recv()

            @pl.when(sends_side(h))
            def _():
                passed(v, h, n).start()

        each_active(one)

    each_active(pass_first)

    for v in range(2):
        @pl.when(jnp.logical_not(active[v]))
        def _(v=v):
            @pl.loop(0, 2 * parts)
            def _(n):
                mine = orbitals_of((OWN,), n // 2, start_of(v, n % 2), quarter)
                local[0] += row_dot(mine, mine)

    groups = basis // 8

    def full_groups(first, end):
        @pl.loop(first, end)
        def _(group):
            left_side = jnp.concatenate([dens_half[group * 8 + k] for k in range(8)], axis=1)
            right_side = jnp.concatenate(
                [
                    coef[:, pl.ds(pl.multiple_of((group * 8 + k) * basis, basis), basis)]
                    for k in range(8)
                ],
                axis=0,
            )
            local[1] += jnp.dot(left_side, right_side, preferred_element_type=jnp.float32)

    ahead = subs - LAG

    @pl.loop(0, ahead)
    def _(n):
        pass_on(1, n)

    full_groups(0, groups // 2)

    @pl.loop(ahead, subs - 1)
    def _(n):
        pass_on(1, n)

    full_groups(groups // 2, groups)
    pass_on(1, subs - 1)

    rows_out = basis // 2
    theirs = pl.multiple_of((1 - a) * rows_out, rows_out)
    ours = pl.multiple_of(a * rows_out, rows_out)

    def to_partner(source, target, which):
        return pltpu.make_async_remote_copy(
            src_ref=source,
            dst_ref=target,
            send_sem=aux_send.at[which],
            recv_sem=aux_recv.at[which],
            device_id=partner,
            device_id_type=MESH,
        )

    swap_local = to_partner(local.at[:, pl.ds(theirs, rows_out)], aux_local, 6)
    swap_local.start()

    def fold(value):
        return value.reshape(2, basis, 2 * basis)

    def gram_of(h, n):
        def one(v):
            part, o = place(h, n)
            here = orbitals_of((OWN, VERT), part, start_of(v, h) + o, size)
            gram[v] += fold(row_dot(here, here))

        each_active(one)

    def products(h, n):
        def one(v):
            @pl.when(gets_side(h))
            def _():
                passed(v, h, n).wait_recv()
                part, o = place(h, n)
                near = orbitals_of((OWN, VERT), part, start_of(v, h) + o, size)
                there = orbitals_of((SIDE, SIDEV), part, start_of(v, h) + o, size)
                acc[v, h, 0] += fold(row_dot(near, there))
                acc[v, h, 1] += fold(row_dot(there, near))

        each_active(one)

    def first_gram(v):
        here = orbitals_of((OWN, VERT), 0, start_of(v, 0), quarter)
        gram[v] = fold(row_dot(here, here))

    def wait_sides(h):
        def one(v):
            @pl.when(gets_side(h))
            def _():
                sideways_all(v, h).wait_recv()

        each_active(one)

    def first_products(v):
        @pl.when(gets_side(0))
        def _():
            passed_first(v).wait_recv()
            near = orbitals_of((OWN, VERT), 0, start_of(v, 0), quarter)
            there = orbitals_of((SIDE, SIDEV), 0, start_of(v, 0), quarter)
            acc[v, 0, 0] = fold(row_dot(near, there))
            acc[v, 0, 1] = fold(row_dot(there, near))

    def clear(v):
        acc[v, 1] = jnp.zeros(acc.shape[2:], jnp.float32)

    each_active(first_gram)
    each_active(clear)
    wait_sides(1)

    @pl.loop(0, numbers[0])
    def _(n):
        pass_on(0, n)
        gram_of(0, n)
        gram_of(1, n)

        @pl.when(n > 0)
        def _():
            products(1, n - 1)

    def pass_late(n):
        pass_on(1, n)
        gram_of(1, n)

    late = numbers[0]
    pass_late(late)
    products(1, late - 1)
    wait_sides(0)
    each_active(first_products)

    @pl.loop(late + 1, numbers[1])
    def _(n):
        pass_late(n)
        products(0, n - late - 1)

        @pl.when(n >= late + LAG)
        def _():
            products(1, n - LAG)

    products(0, numbers[0] - 1)

    def swap_acc(v, h):
        return to_partner(
            acc.at[v, h, :, :, pl.ds(theirs, rows_out)], aux_acc.at[v, h], 2 * slot(v) + h
        )

    def swap_gram(v):
        return to_partner(
            gram.at[v, :, pl.ds(theirs, rows_out)], aux_gram.at[v], 4 + slot(v)
        )

    has = [both(active[v], gets_side(h)) for v, h in ROLES]

    def box(v, h, kind):
        row, col = r + 1 - 2 * v, c - 1 + 2 * h
        device = ({"row": row}, {"col": col}, {"row": row, "col": col})[kind]
        return pltpu.make_async_remote_copy(
            src_ref=outbox.at[v, h, kind],
            dst_ref=inbox.at[v, h, kind],
            send_sem=box_send.at[slot(v), h],
            recv_sem=box_recv.at[kind, slot(v), h],
            device_id=device,
            device_id_type=MESH,
        )

    def box_all(v, h):
        return pltpu.make_async_remote_copy(
            src_ref=outbox.at[v, h],
            dst_ref=inbox.at[v, h],
            send_sem=box_send.at[slot(v), h],
            recv_sem=box_recv.at[0, slot(v), h],
            device_id=partner,
            device_id_type=MESH,
        )

    def box_v(v):
        return pltpu.make_async_remote_copy(
            src_ref=outbox_v.at[v],
            dst_ref=inbox_v.at[v],
            send_sem=boxv_send.at[slot(v)],
            recv_sem=boxv_recv.at[slot(v)],
            device_id=vert_from[v],
            device_id_type=MESH,
        )

    def swap_sums(h):
        for v in range(2):
            @pl.when(both(active[v], gets_side(h)))
            def _(v=v):
                swap_acc(v, h).start()

    def send_boxes(h):
        for v in range(2):
            @pl.when(both(active[v], gets_side(h)))
            def _(v=v):
                swap_acc(v, h).wait_recv()
                for side, half in ((0, 1), (1, 1), (1, 0)):
                    kind = 2 * side + half - 1
                    outbox[v, h, kind] = (
                        acc[v, h, side, half, pl.ds(ours, rows_out), :]
                        + aux_acc[v, h, side, half]
                    ).astype(outbox.dtype)
                    box(v, h, kind).start()

    swap_sums(0)
    for v in range(2):
        @pl.when(active[v])
        def _(v=v):
            swap_gram(v).start()

    arrives = [
        (
            both(up_down[v], (left, right)[h]),
            both(active[v], (right, left)[h]),
            both(up_down[v], (right, left)[h]),
        )
        for v, h in ROLES
    ]
    for index, (v, h) in enumerate(ROLES):
        for kind in range(3):
            @pl.when(jnp.logical_not(arrives[index][kind]))
            def _(v=v, h=h, kind=kind):
                inbox[v, h, kind] = jnp.zeros(inbox.shape[3:], inbox.dtype)

        @pl.when(jnp.logical_not(has[index]))
        def _(v=v, h=h):
            zeros = jnp.zeros((rows_out, 2 * basis), jnp.float32)
            acc[v, h, 0, 0, pl.ds(ours, rows_out), :] = zeros
            aux_acc[v, h, 0, 0] = zeros
    for v in range(2):
        @pl.when(jnp.logical_not(up_down[v]))
        def _(v=v):
            inbox_v[v] = jnp.zeros(inbox_v.shape[1:], inbox_v.dtype)

        @pl.when(jnp.logical_not(active[v]))
        def _(v=v):
            zeros = jnp.zeros((rows_out, 2 * basis), jnp.float32)
            gram[v, 0, pl.ds(ours, rows_out), :] = zeros
            aux_gram[v, 0] = zeros

    for v in range(2):
        @pl.when(up_down[v])
        def _(v=v):
            vertical_all(v).wait_send()

    @pl.loop(numbers[1] - LAG, numbers[1] - 2)
    def _(n):
        products(1, n)

    send_boxes(0)
    for v in range(2):
        @pl.when(active[v])
        def _(v=v):
            swap_gram(v).wait_recv()
            outbox_v[v] = (
                gram[v, 1, pl.ds(ours, rows_out), :basis] + aux_gram[v, 1, :, :basis]
            ).astype(outbox_v.dtype)
            box_v(v).start()

    @pl.loop(numbers[1] - 2, numbers[1])
    def _(n):
        products(1, n)

    swap_sums(1)
    for v, h in ROLES:
        @pl.when(both(active[v], sends_side(h)))
        def _(v=v, h=h):
            sideways_all(v, h).wait_send()
            passed_all(v, h).wait_send()

    send_boxes(1)

    total = [None] * 8

    def add(d, value):
        total[d] = value if total[d] is None else total[d] + value

    swap_local.wait_recv()
    own = local[0, pl.ds(ours, rows_out), :] + aux_local[0]
    out_ref[9] = local[1, pl.ds(ours, rows_out), :] + aux_local[1]
    for v in range(2):
        value = gram[v, 0, pl.ds(ours, rows_out), :] + aux_gram[v, 0]
        own = own + value[:, :basis]
        add((6, 1)[v], value[:, basis:])
    out_ref[8] = own

    far = ((5, 7), (0, 2))
    for index, (v, h) in enumerate(ROLES):
        value = acc[v, h, 0, 0, pl.ds(ours, rows_out), :] + aux_acc[v, h, 0, 0]
        add((3, 4)[h], value[:, :basis])
        add(far[v][h], value[:, basis:])

    for v in range(2):
        @pl.when(up_down[v])
        def _(v=v):
            box_v(v).wait_recv()

        add((1, 6)[v], inbox_v[v].astype(jnp.float32))

    last = (jnp.logical_not(below), jnp.logical_not(above))
    for index, (v, h) in enumerate(ROLES):
        for kind in range(3):
            @pl.when(arrives[index][kind])
            def _(v=v, h=h, kind=kind):
                box(v, h, kind).wait_recv()

        vert, side, diag = (inbox[v, h, kind].astype(jnp.float32) for kind in range(3))
        edge = last[v].astype(jnp.float32)
        add(far[1 - v][h], vert[:, :basis])
        add((3, 4)[h], vert[:, basis:] * edge)
        add((4, 3)[h], side[:, :basis])
        add(far[v][1 - h], side[:, basis:])
        add(far[1 - v][1 - h], diag[:, :basis])
        add((4, 3)[h], diag[:, basis:] * edge)
    for d in range(8):
        out_ref[d] = total[d]

    for index, (v, h) in enumerate(ROLES):
        @pl.when(has[index])
        def _(v=v, h=h):
            swap_acc(v, h).wait_send()
            box_all(v, h).wait_send()
    for v in range(2):
        @pl.when(active[v])
        def _(v=v):
            swap_gram(v).wait_send()
            box_v(v).wait_send()
    swap_local.wait_send()


def finish_kernel(scales, sums_ref, mask_ref, self_ref, pair_ref, full_ref):
    self_scale, pair_scale, full_scale = scales
    for d in range(8):
        factor = mask_ref[d].astype(jnp.float32)
        pair_ref[0, 0, d] = sums_ref[d] * pair_scale * factor
    self_ref[0, 0] = sums_ref[8] * self_scale
    full_ref[0, 0] = sums_ref[9] * full_scale


def local_step(rows, cols, aux, coef_three, orbitals, density, pair_mask):
    q_local, width = coef_three.shape[2:]
    occ, basis = orbitals.shape[2:]
    coef = coef_three[0, 0]
    q_total = q_local * aux
    scales = (
        1.0 / (q_total * occ), 1.0 / (q_total * occ) ** 0.5, 1.0 / (q_total * basis) ** 0.5
    )
    rows_out = basis // aux
    lanes = 128
    parts = q_local // lanes
    subs = chunks_of(occ)[2]
    chunks = (2 * parts - 1) * subs
    sets = 1 if rows == 2 else 2
    f32, bf16 = jnp.float32, jnp.bfloat16
    dma = pltpu.SemaphoreType.DMA
    vmem = pl.BlockSpec(memory_space=pltpu.VMEM)
    sums = pl.pallas_call(
        functools.partial(exchange_kernel, rows, cols),
        out_shape=jax.ShapeDtypeStruct((10, rows_out, basis), f32),
        in_specs=[
            pl.BlockSpec(memory_space=pl.ANY),
            pl.BlockSpec(memory_space=pl.ANY),
            pl.BlockSpec(memory_space=pl.ANY),
        ],
        out_specs=vmem,
        scratch_shapes=[
            pltpu.VMEM((4, parts, occ, basis, lanes), bf16),
            pltpu.VMEM((q_local, width), bf16),
            pltpu.VMEM((occ, basis), bf16),
            pltpu.VMEM((basis, basis), bf16),
            pltpu.VMEM((parts, BLOCK * max(odd_tiles(basis), odd_tiles(occ)), lanes), f32),
            pltpu.VMEM((basis, basis, q_local), bf16),
            pltpu.VMEM((2, 2, 2, 2, basis, 2 * basis), f32),
            pltpu.VMEM((2, 2, basis, 2 * basis), f32),
            pltpu.VMEM((2, basis, basis), f32),
            pltpu.VMEM((2, 2, 3, rows_out, 2 * basis), WIRE),
            pltpu.VMEM((2, rows_out, basis), WIRE),
            pltpu.VMEM((2, 2, 3, rows_out, 2 * basis), WIRE),
            pltpu.VMEM((2, rows_out, basis), WIRE),
            pltpu.VMEM((2, 2, 2, 2, rows_out, 2 * basis), f32),
            pltpu.VMEM((2, 2, rows_out, 2 * basis), f32),
            pltpu.VMEM((2, rows_out, basis), f32),
            dma((parts, CUTS)),
            dma((2,)),
            dma((sets,)),
            dma((sets, 1 + chunks)),
            dma((sets, 2)),
            dma((sets, 2)),
            dma((sets, 2)),
            dma((sets, 1 + chunks)),
            dma((sets, 2)),
            dma((3, sets, 2)),
            dma((sets,)),
            dma((sets,)),
            dma((7,)),
            dma((7,)),
        ],
        compiler_params=pltpu.CompilerParams(
            collective_id=0, has_side_effects=True, vmem_limit_bytes=56 << 20
        ),
        name="exchange",
    )(coef, orbitals[0, 0], density[0, 0])
    return pl.pallas_call(
        functools.partial(finish_kernel, scales),
        out_shape=(
            jax.ShapeDtypeStruct((1, 1, rows_out, basis), f32),
            jax.ShapeDtypeStruct((1, 1, 8, rows_out, basis), f32),
            jax.ShapeDtypeStruct((1, 1, rows_out, basis), f32),
        ),
        in_specs=[vmem, pl.BlockSpec(memory_space=pltpu.SMEM)],
        out_specs=(vmem, vmem, vmem),
        name="finish",
    )(sums, pair_mask[0, 0])


def solution(mesh):
    in_specs = (
        P(("sys", "row"), "col", "aux", None),
        P(("sys", "row"), "col", None, None),
        P(("sys", "row"), "col", None, None),
        P(("sys", "row"), "col", None),
    )
    out_specs = (
        P(("sys", "row"), "col", "aux", None),
        P(("sys", "row"), "col", None, "aux", None),
        P(("sys", "row"), "col", "aux", None),
    )
    body = functools.partial(local_step, mesh.shape["row"], mesh.shape["col"], mesh.shape["aux"])
    return jax.shard_map(body, mesh=mesh, in_specs=in_specs, out_specs=out_specs, check_vma=False)
```

time: 54.7 us -> 45.1 us (0.82)
  the two profiles are of different devices: /device:TPU:17 before, /device:TPU:1 now
where the time goes in v2:
time: 45.1 us; the launch traced here: 44.9 us
  Pallas kernels  44.2 us (98%)
  between operations  0.64 us (1%)
    pallas_call x1, Pallas kernels, local_step(): pl.pallas_call(functools.partial(exchange_kernel, rows, cols), out_shape=...  42.5 us
    pallas_call x1, Pallas kernels, local_step(): pl.pallas_call(functools.partial(finish_kernel, scales), out_shape=(jax.S...  1.72 us

profile of v2, /device:TPU:1, one launch (start us, length us, event | category | flops | bytes accessed | tf_op | source)
XLA Modules:
  0.0 44.9 jit_solution(2217019884214459876)
XLA Ops:
  0.6 42.5 %exchange.1.sums_ref = f32[10,64,128]{2,1,0:T(8,128)} custom-call(bf16[256,16384]{1,0:T(8,128)(2,1)} %bitcast.4, bf16[40,128]{1,0:T(8,128)(2,1)} %bitcast.6, bf16[128,128]{1,0:T(8,128)(2,1)} %bitcast.5), custom_call_target="tpu_custom_call" | custom-call | tf_op jit(solution)/shard_map/exchange/pallas_call | solution.py:642
  43.2 1.7 %finish.1 = (f32[1,1,64,128]{3,2,1,0:T(8,128)}, f32[1,1,8,64,128]{4,3,2,1,0:T(8,128)}, f32[1,1,64,128]{3,2,1,0:T(8,128)}) custom-call(f32[10,64,128]{2,1,0:T(8,128)} %exchange.1.sums_ref, s32[8]{0:T(128)} %bitcast.7), custom_call_target="tpu_custom_call" | custom-call | tf_op jit(solution)/shard_map/finish/pallas_call | solution.py:688

commit v3 on v2

--- a/solution.py
+++ b/solution.py
@@ -11,7 +11,8 @@
 OWN, VERT, SIDE, SIDEV = range(4)
 ROLES = ((0, 0), (0, 1), (1, 0), (1, 1))
 BLOCK = 16
-CUTS = 4
+CUTS = (0, 1, 2, 4, 8)
+PIECES = len(CUTS) - 1
 LAG = 3
 WIRE = jnp.bfloat16
 
@@ -34,8 +35,8 @@
 
 
 def exchange_kernel(
-    rows, cols, coef_hbm, orb_hbm, dens_hbm, out_ref,
-    blocks, coef, orb_ref, dens_ref, stage, dens_half, acc, gram, local,
+    rows, cols, scales, coef_hbm, orb_hbm, dens_hbm, mask_hbm, out_ref,
+    blocks, coef, orb_ref, dens_ref, mask_ref, stage, dens_half, acc, gram, local,
     outbox, outbox_v, inbox, inbox_v, aux_acc, aux_gram, aux_local,
     load_sem, small_sem, vert_send, vert_recv, side_send, side_recv, pass_send, pass_recv,
     box_send, box_recv, boxv_send, boxv_recv, aux_send, aux_recv,
@@ -47,7 +48,6 @@
     both = jnp.logical_and
     parts, lanes = blocks.shape[1], blocks.shape[4]
     steps = basis // BLOCK
-    width = coef.shape[1]
     quarter, size, subs = chunks_of(occ)
     numbers = ((parts - 1) * subs, parts * subs)
 
@@ -57,16 +57,19 @@
     first_v = jnp.where(below, 0, 1)
     end_v = jnp.where(above, 2, 1)
 
-    span = width // CUTS
+    def cut(k):
+        return CUTS[k] * basis // CUTS[-1], (CUTS[k + 1] - CUTS[k]) * basis // CUTS[-1]
 
     def load(part, k):
-        piece = (pl.ds(part * lanes, lanes), pl.ds(pl.multiple_of(k * span, span), span))
+        first, number = cut(k)
+        piece = (pl.ds(part * lanes, lanes), pl.ds(first * basis, number * basis))
         return pltpu.make_async_copy(
             coef_hbm.at[piece], coef.at[piece], load_sem.at[part, k]
         )
 
     load_orb = pltpu.make_async_copy(orb_hbm, orb_ref, small_sem.at[0])
     load_dens = pltpu.make_async_copy(dens_hbm, dens_ref, small_sem.at[1])
+    load_mask = pltpu.make_async_copy(mask_hbm, mask_ref, small_sem.at[2])
     load_orb.start()
     load(0, 0).start()
 
@@ -111,8 +114,6 @@
             device_id_type=MESH,
         )
 
-    cut = basis // CUTS
-
     def start_of(v, h):
         return v * (2 * quarter) + h * quarter
 
@@ -124,7 +125,7 @@
         return copy(OWN, SIDE, piece, side_send.at[pair], side_recv.at[pair], side_of(h))
 
     def sideways_cut(v, h, k):
-        return sideways(v, h, (0, pl.ds(start_of(v, h), quarter), pl.ds(k * cut, cut)))
+        return sideways(v, h, (0, pl.ds(start_of(v, h), quarter), pl.ds(*cut(k))))
 
     def sideways_part(v, h, part):
         return sideways(v, h, (part, pl.ds(start_of(v, h), quarter)))
@@ -137,7 +138,7 @@
         return copy(OWN, VERT, piece, send, recv, row_of(v))
 
     def vertical_cut(v, k):
-        return up_or_down(v, (0, pl.ds(start_of(v, 0), quarter), pl.ds(k * cut, cut)), 0)
+        return up_or_down(v, (0, pl.ds(start_of(v, 0), quarter), pl.ds(*cut(k))), 0)
 
     def vertical_first(v):
         return up_or_down(v, (0, pl.ds(start_of(v, 0), quarter)), 0)
@@ -155,6 +156,15 @@
     def vertical(v, h, n):
         return up_or_down(v, chunk(v, h, n), 1 + h * numbers[0] + n)
 
+    final = numbers[1] - 1
+    tail = [(final + i, start_of(0, 1) + (subs - 1) * size + i) for i in range(size)]
+
+    def tail_piece(v, o):
+        return parts - 1, pl.ds(v * (2 * quarter) + o, 1)
+
+    def vertical_tail(v, n, o):
+        return up_or_down(v, tail_piece(v, o), 1 + numbers[0] + n)
+
     def pass_piece(v, h, piece, k):
         send, recv = pass_send.at[slot(v), h], pass_recv.at[slot(v), k]
         return copy(VERT, SIDEV, piece, send, recv, side_of(h))
@@ -164,6 +174,9 @@
 
     def passed(v, h, n):
         return pass_piece(v, h, chunk(v, h, n), 1 + h * numbers[0] + n)
+
+    def passed_tail(v, n, o):
+        return pass_piece(v, 1, tail_piece(v, o), 1 + numbers[0] + n)
 
     def passed_all(v, h):
         return pass_piece(v, h, (slice(None), pl.ds(start_of(v, h), quarter)), 0)
@@ -175,10 +188,11 @@
 
     load_orb.wait()
     for part in range(parts):
-        for k in range(CUTS):
+        for k in range(PIECES):
             if part + k > 0:
                 load(part, k).start()
     load_dens.start()
+    load_mask.start()
     orb = orb_ref[...]
     zero = jnp.zeros_like(orb)
     two = jnp.concatenate(
@@ -186,13 +200,12 @@
     )
     pitch = odd_tiles(occ)
 
-    def half_transform(part, first_step, end_step):
-        @pl.loop(first_step, end_step)
+    def half_transform(part, k):
+        first_basis, number = cut(k)
+        load(part, k).wait()
+
+        @pl.loop(first_basis // BLOCK, (first_basis + number) // BLOCK)
         def _(step):
-            @pl.when(step % (steps // CUTS) == 0)
-            def _():
-                load(part, step // (steps // CUTS)).wait()
-
             for m in range(0, BLOCK, 2):
                 at = pl.multiple_of((step * BLOCK + m) * basis, 2 * basis)
                 value = row_dot(
@@ -206,8 +219,8 @@
                 piece = stage[part, pl.ds(o, BLOCK, stride=pitch), :]
                 blocks[OWN, part, o, pl.ds(first, BLOCK), :] = piece.astype(jnp.bfloat16)
 
-    for k in range(CUTS):
-        half_transform(0, k * steps // CUTS, (k + 1) * steps // CUTS)
+    for k in range(PIECES):
+        half_transform(0, k)
         if k == 0:
             pl.semaphore_wait(barrier, expected)
         for v in range(2):
@@ -229,15 +242,23 @@
 
     start_vertical(1, 0, subs)
     for part in range(1, parts):
-        half_transform(part, 0, steps)
+        for k in range(PIECES):
+            half_transform(part, k)
         start_vertical(0, (part - 1) * subs, part * subs)
-        start_vertical(1, part * subs, (part + 1) * subs)
+        start_vertical(1, part * subs, (part + 1) * subs - (1 if part == parts - 1 else 0))
+        if part == parts - 1:
+            for v in range(2):
+                @pl.when(up_down[v])
+                def _(v=v):
+                    for n, o in tail:
+                        vertical_tail(v, n, o).start()
         for v, h in ROLES:
             @pl.when(both(active[v], sends_side(h)))
             def _(v=v, h=h, part=part):
                 sideways_part(v, h, part).start()
     local[...] = jnp.zeros(local.shape, jnp.float32)
     load_dens.wait()
+    load_mask.wait()
     dens_turned = dens_ref[...].astype(jnp.float32).T.astype(jnp.bfloat16)
     wide = odd_tiles(basis)
 
@@ -413,7 +434,7 @@
     wait_sides(0)
     each_active(first_products)
 
-    @pl.loop(late + 1, numbers[1])
+    @pl.loop(late + 1, final)
     def _(n):
         pass_late(n)
         products(0, n - late - 1)
@@ -422,6 +443,36 @@
         def _():
             products(1, n - LAG)
 
+    def pass_tail(n, o):
+        def one(v):
+            vertical_tail(v, n, o).wait_recv()
+
+            @pl.when(sends_side(1))
+            def _():
+                passed_tail(v, n, o).start()
+
+            here = orbitals_of((OWN, VERT), parts - 1, v * (2 * quarter) + o, 1)
+            gram[v] += fold(row_dot(here, here))
+
+        each_active(one)
+
+    def products_tail(n, o):
+        def one(v):
+            @pl.when(gets_side(1))
+            def _():
+                passed_tail(v, n, o).wait_recv()
+                near = orbitals_of((OWN, VERT), parts - 1, v * (2 * quarter) + o, 1)
+                there = orbitals_of((SIDE, SIDEV), parts - 1, v * (2 * quarter) + o, 1)
+                acc[v, 1, 0] += fold(row_dot(near, there))
+                acc[v, 1, 1] += fold(row_dot(there, near))
+
+        each_active(one)
+
+    pass_tail(*tail[0])
+    products(0, final - late - 1)
+    products(1, final - LAG)
+    for n, o in tail[1:]:
+        pass_tail(n, o)
     products(0, numbers[0] - 1)
 
     def swap_acc(v, h):
@@ -479,7 +530,7 @@
             @pl.when(both(active[v], gets_side(h)))
             def _(v=v):
                 swap_acc(v, h).wait_recv()
-                for side, half in ((0, 1), (1, 1), (1, 0)):
+                for side, half in ((1, 1), (0, 1), (1, 0)):
                     kind = 2 * side + half - 1
                     outbox[v, h, kind] = (
                         acc[v, h, side, half, pl.ds(ours, rows_out), :]
@@ -528,7 +579,7 @@
         def _(v=v):
             vertical_all(v).wait_send()
 
-    @pl.loop(numbers[1] - LAG, numbers[1] - 2)
+    @pl.loop(final - LAG + 1, final - 1)
     def _(n):
         products(1, n)
 
@@ -542,10 +593,9 @@
             ).astype(outbox_v.dtype)
             box_v(v).start()
 
-    @pl.loop(numbers[1] - 2, numbers[1])
-    def _(n):
-        products(1, n)
-
+    products(1, final - 1)
+    for n, o in tail:
+        products_tail(n, o)
     swap_sums(1)
     for v, h in ROLES:
         @pl.when(both(active[v], sends_side(h)))
@@ -555,6 +605,7 @@
 
     send_boxes(1)
 
+    self_scale, pair_scale, full_scale = scales
     total = [None] * 8
 
     def add(d, value):
@@ -562,12 +613,12 @@
 
     swap_local.wait_recv()
     own = local[0, pl.ds(ours, rows_out), :] + aux_local[0]
-    out_ref[9] = local[1, pl.ds(ours, rows_out), :] + aux_local[1]
+    out_ref[9] = (local[1, pl.ds(ours, rows_out), :] + aux_local[1]) * full_scale
     for v in range(2):
         value = gram[v, 0, pl.ds(ours, rows_out), :] + aux_gram[v, 0]
         own = own + value[:, :basis]
         add((6, 1)[v], value[:, basis:])
-    out_ref[8] = own
+    out_ref[8] = own * self_scale
 
     far = ((5, 7), (0, 2))
     for index, (v, h) in enumerate(ROLES):
@@ -598,7 +649,7 @@
         add(far[1 - v][1 - h], diag[:, :basis])
         add((4, 3)[h], diag[:, basis:] * edge)
     for d in range(8):
-        out_ref[d] = total[d]
+        out_ref[d] = total[d] * (pair_scale * mask_ref[d].astype(jnp.float32))
 
     for index, (v, h) in enumerate(ROLES):
         @pl.when(has[index])
@@ -613,13 +664,16 @@
     swap_local.wait_send()
 
 
-def finish_kernel(scales, sums_ref, mask_ref, self_ref, pair_ref, full_ref):
-    self_scale, pair_scale, full_scale = scales
-    for d in range(8):
-        factor = mask_ref[d].astype(jnp.float32)
-        pair_ref[0, 0, d] = sums_ref[d] * pair_scale * factor
-    self_ref[0, 0] = sums_ref[8] * self_scale
-    full_ref[0, 0] = sums_ref[9] * full_scale
+def finish_kernel(sums_ref, self_ref, pair_ref, full_ref, sem):
+    copies = [
+        pltpu.make_async_copy(sums_ref.at[pl.ds(0, 8)], pair_ref.at[0, 0], sem.at[0]),
+        pltpu.make_async_copy(sums_ref.at[8], self_ref.at[0, 0], sem.at[1]),
+        pltpu.make_async_copy(sums_ref.at[9], full_ref.at[0, 0], sem.at[2]),
+    ]
+    for copy in copies:
+        copy.start()
+    for copy in copies:
+        copy.wait()
 
 
 def local_step(rows, cols, aux, coef_three, orbitals, density, pair_mask):
@@ -633,26 +687,24 @@
     rows_out = basis // aux
     lanes = 128
     parts = q_local // lanes
-    subs = chunks_of(occ)[2]
+    _, size, subs = chunks_of(occ)
     chunks = (2 * parts - 1) * subs
     sets = 1 if rows == 2 else 2
     f32, bf16 = jnp.float32, jnp.bfloat16
     dma = pltpu.SemaphoreType.DMA
     vmem = pl.BlockSpec(memory_space=pltpu.VMEM)
+    anywhere = pl.BlockSpec(memory_space=pl.ANY)
     sums = pl.pallas_call(
-        functools.partial(exchange_kernel, rows, cols),
-        out_shape=jax.ShapeDtypeStruct((10, rows_out, basis), f32),
-        in_specs=[
-            pl.BlockSpec(memory_space=pl.ANY),
-            pl.BlockSpec(memory_space=pl.ANY),
-            pl.BlockSpec(memory_space=pl.ANY),
-        ],
+        functools.partial(exchange_kernel, rows, cols, scales),
+        out_shape=pltpu.VMEM((10, rows_out, basis), f32),
+        in_specs=[anywhere] * 4,
         out_specs=vmem,
         scratch_shapes=[
             pltpu.VMEM((4, parts, occ, basis, lanes), bf16),
             pltpu.VMEM((q_local, width), bf16),
             pltpu.VMEM((occ, basis), bf16),
             pltpu.VMEM((basis, basis), bf16),
+            pltpu.SMEM((8,), jnp.int32),
             pltpu.VMEM((parts, BLOCK * max(odd_tiles(basis), odd_tiles(occ)), lanes), f32),
             pltpu.VMEM((basis, basis, q_local), bf16),
             pltpu.VMEM((2, 2, 2, 2, basis, 2 * basis), f32),
@@ -665,14 +717,14 @@
             pltpu.VMEM((2, 2, 2, 2, rows_out, 2 * basis), f32),
             pltpu.VMEM((2, 2, rows_out, 2 * basis), f32),
             pltpu.VMEM((2, rows_out, basis), f32),
-            dma((parts, CUTS)),
-            dma((2,)),
+            dma((parts, PIECES)),
+            dma((3,)),
             dma((sets,)),
-            dma((sets, 1 + chunks)),
+            dma((sets, chunks + size)),
             dma((sets, 2)),
             dma((sets, 2)),
             dma((sets, 2)),
-            dma((sets, 1 + chunks)),
+            dma((sets, chunks + size)),
             dma((sets, 2)),
             dma((3, sets, 2)),
             dma((sets,)),
@@ -684,18 +736,19 @@
             collective_id=0, has_side_effects=True, vmem_limit_bytes=56 << 20
         ),
         name="exchange",
-    )(coef, orbitals[0, 0], density[0, 0])
+    )(coef, orbitals[0, 0], density[0, 0], pair_mask[0, 0])
     return pl.pallas_call(
-        functools.partial(finish_kernel, scales),
+        finish_kernel,
         out_shape=(
             jax.ShapeDtypeStruct((1, 1, rows_out, basis), f32),
             jax.ShapeDtypeStruct((1, 1, 8, rows_out, basis), f32),
             jax.ShapeDtypeStruct((1, 1, rows_out, basis), f32),
         ),
-        in_specs=[vmem, pl.BlockSpec(memory_space=pltpu.SMEM)],
-        out_specs=(vmem, vmem, vmem),
+        in_specs=[vmem],
+        out_specs=(anywhere, anywhere, anywhere),
+        scratch_shapes=[dma((3,))],
         name="finish",
-    )(sums, pair_mask[0, 0])
+    )(pltpu.with_memory_space_constraint(sums, pltpu.VMEM))
 
 
 def solution(mesh):

time: 45.1 us -> 44 us (0.976)
  Pallas kernels: 44.2 us -> 43.2 us
    pallas_call x2, Pallas kernels: 44.2 us -> 43.2 us  [the longest x1 42.4 us: local_step(): pl.pallas_call(functools.partial(exchange_kernel, rows, cols, scales), ou...]
where the time goes in v3:
time: 44 us; the launch traced here: 43.8 us
  Pallas kernels  43.2 us (98%)
  between operations  0.64 us (1%)
    pallas_call x1, Pallas kernels, local_step(): pl.pallas_call(functools.partial(exchange_kernel, rows, cols, scales), ou...  42.4 us

profile of v3, /device:TPU:1, one launch (start us, length us, event | category | flops | bytes accessed | tf_op | source)
XLA Modules:
  0.0 43.8 jit_solution(16532831467752899542)
XLA Ops:
  0.6 42.4 %exchange.1.sums_ref = f32[10,64,128]{2,1,0:T(8,128)S(1)} custom-call(bf16[256,16384]{1,0:T(8,128)(2,1)} %bitcast.4, bf16[40,128]{1,0:T(8,128)(2,1)} %bitcast.6, bf16[128,128]{1,0:T(8,128)(2,1)} %bitcast.5, s32[8]{0:T(128)} %bitcast.7), custom_call_target="tpu_custom_call" | custom-call | tf_op jit(solution)/shard_map/exchange/pallas_call | solution.py:697
  43.1 0.7 %finish.1 = (f32[1,1,64,128]{3,2,1,0:T(8,128)}, f32[1,1,8,64,128]{4,3,2,1,0:T(8,128)}, f32[1,1,64,128]{3,2,1,0:T(8,128)}) custom-call(f32[10,64,128]{2,1,0:T(8,128)S(1)} %exchange.1.sums_ref), custom_call_target="tpu_custom_call" | custom-call | tf_op jit(solution)/shard_map/finish/pallas_call | solution.py:740

commit v4 on v3

--- a/solution.py
+++ b/solution.py
@@ -13,7 +13,7 @@
 BLOCK = 16
 CUTS = (0, 1, 2, 4, 8)
 PIECES = len(CUTS) - 1
-LAG = 3
+LEAD = 3
 WIRE = jnp.bfloat16
 
 
@@ -240,16 +240,23 @@
                 def _(n):
                     vertical(v, h, n).start()
 
+    rest = [(1, n) for n in range(subs, final)]
+    order = [(0, n) for n in range(LEAD)]
+    for n in range(LEAD, numbers[0]):
+        order += rest[:1] + [(0, n)]
+        rest = rest[1:]
+    order += rest
+
     start_vertical(1, 0, subs)
     for part in range(1, parts):
         for k in range(PIECES):
             half_transform(part, k)
-        start_vertical(0, (part - 1) * subs, part * subs)
-        start_vertical(1, part * subs, (part + 1) * subs - (1 if part == parts - 1 else 0))
         if part == parts - 1:
             for v in range(2):
                 @pl.when(up_down[v])
                 def _(v=v):
+                    for h, n in order:
+                        vertical(v, h, n).start()
                     for n, o in tail:
                         vertical_tail(v, n, o).start()
         for v, h in ROLES:
@@ -330,7 +337,7 @@
             )
             local[1] += jnp.dot(left_side, right_side, preferred_element_type=jnp.float32)
 
-    ahead = subs - LAG
+    ahead = 2
 
     @pl.loop(0, ahead)
     def _(n):
@@ -365,24 +372,10 @@
     def fold(value):
         return value.reshape(2, basis, 2 * basis)
 
-    def gram_of(h, n):
+    def gram_span(h, part, first, number):
         def one(v):
-            part, o = place(h, n)
-            here = orbitals_of((OWN, VERT), part, start_of(v, h) + o, size)
+            here = orbitals_of((OWN, VERT), part, start_of(v, h) + first, number)
             gram[v] += fold(row_dot(here, here))
-
-        each_active(one)
-
-    def products(h, n):
-        def one(v):
-            @pl.when(gets_side(h))
-            def _():
-                passed(v, h, n).wait_recv()
-                part, o = place(h, n)
-                near = orbitals_of((OWN, VERT), part, start_of(v, h) + o, size)
-                there = orbitals_of((SIDE, SIDEV), part, start_of(v, h) + o, size)
-                acc[v, h, 0] += fold(row_dot(near, there))
-                acc[v, h, 1] += fold(row_dot(there, near))
 
         each_active(one)
 
@@ -410,38 +403,24 @@
     def clear(v):
         acc[v, 1] = jnp.zeros(acc.shape[2:], jnp.float32)
 
-    each_active(first_gram)
-    each_active(clear)
-    wait_sides(1)
-
-    @pl.loop(0, numbers[0])
-    def _(n):
-        pass_on(0, n)
-        gram_of(0, n)
-        gram_of(1, n)
-
-        @pl.when(n > 0)
-        def _():
-            products(1, n - 1)
-
-    def pass_late(n):
-        pass_on(1, n)
-        gram_of(1, n)
-
-    late = numbers[0]
-    pass_late(late)
-    products(1, late - 1)
-    wait_sides(0)
-    each_active(first_products)
-
-    @pl.loop(late + 1, final)
-    def _(n):
-        pass_late(n)
-        products(0, n - late - 1)
-
-        @pl.when(n >= late + LAG)
-        def _():
-            products(1, n - LAG)
+    def products_span(h, first, end):
+        def one(v):
+            @pl.when(gets_side(h))
+            def _():
+                at = first
+                while at < end:
+                    stop = min(end, (at // subs + 1) * subs)
+                    for n in range(at, stop):
+                        passed(v, h, n).wait_recv()
+                    part, o = place(h, at)
+                    o, number = start_of(v, h) + o, (stop - at) * size
+                    near = orbitals_of((OWN, VERT), part, o, number)
+                    there = orbitals_of((SIDE, SIDEV), part, o, number)
+                    acc[v, h, 0] += fold(row_dot(near, there))
+                    acc[v, h, 1] += fold(row_dot(there, near))
+                    at = stop
+
+        each_active(one)
 
     def pass_tail(n, o):
         def one(v):
@@ -450,9 +429,6 @@
             @pl.when(sends_side(1))
             def _():
                 passed_tail(v, n, o).start()
-
-            here = orbitals_of((OWN, VERT), parts - 1, v * (2 * quarter) + o, 1)
-            gram[v] += fold(row_dot(here, here))
 
         each_active(one)
 
@@ -468,12 +444,35 @@
 
         each_active(one)
 
-    pass_tail(*tail[0])
-    products(0, final - late - 1)
-    products(1, final - LAG)
-    for n, o in tail[1:]:
+    each_active(first_gram)
+    each_active(clear)
+    wait_sides(1)
+    work = [[(1, n, n + 1)] for n in range(subs)]
+    work[-1].append(None)
+    work += [[(0, 0, 1), (1, subs, subs + 1)], [(0, 1, 2)]]
+
+    def do(items):
+        for item in items:
+            if item is None:
+                wait_sides(0)
+                each_active(first_products)
+            else:
+                products_span(*item)
+
+    for i, (h, n) in enumerate(order):
+        pass_on(h, n)
+        if i == 0:
+            gram_span(1, 0, 0, quarter)
+        if i >= 2 and work:
+            do(work.pop(0))
+        if (h, n) == (0, numbers[0] - 1):
+            for part in range(1, parts):
+                gram_span(0, part, 0, quarter)
+    for n, o in tail:
         pass_tail(n, o)
-    products(0, numbers[0] - 1)
+    for items in work:
+        do(items)
+    products_span(0, 2, numbers[0])
 
     def swap_acc(v, h):
         return to_partner(
@@ -539,6 +538,8 @@
                     box(v, h, kind).start()
 
     swap_sums(0)
+    for part in range(1, parts):
+        gram_span(1, part, 0, quarter)
     for v in range(2):
         @pl.when(active[v])
         def _(v=v):
@@ -579,9 +580,7 @@
         def _(v=v):
             vertical_all(v).wait_send()
 
-    @pl.loop(final - LAG + 1, final - 1)
-    def _(n):
-        products(1, n)
+    products_span(1, subs + 1, final - 1)
 
     send_boxes(0)
     for v in range(2):
@@ -593,7 +592,7 @@
             ).astype(outbox_v.dtype)
             box_v(v).start()
 
-    products(1, final - 1)
+    products_span(1, final - 1, final)
     for n, o in tail:
         products_tail(n, o)
     swap_sums(1)

time: 44 us -> 43.2 us (0.982)
  Pallas kernels: 43.2 us -> 42.4 us
    pallas_call x1, Pallas kernels: 42.4 us -> 41.6 us  [local_step(): pl.pallas_call(functools.partial(exchange_kernel, rows, cols, scales), ou...]
where the time goes in v4:
time: 43.2 us; the launch traced here: 43 us
  Pallas kernels  42.4 us (98%)
  between operations  0.64 us (1%)
    pallas_call x1, Pallas kernels, local_step(): pl.pallas_call(functools.partial(exchange_kernel, rows, cols, scales), ou...  41.6 us

profile of v4, /device:TPU:1, one launch (start us, length us, event | category | flops | bytes accessed | tf_op | source)
XLA Modules:
  0.0 43.0 jit_solution(8977999103728879052)
XLA Ops:
  0.6 41.6 %exchange.1.sums_ref = f32[10,64,128]{2,1,0:T(8,128)S(1)} custom-call(bf16[256,16384]{1,0:T(8,128)(2,1)} %bitcast.4, bf16[40,128]{1,0:T(8,128)(2,1)} %bitcast.6, bf16[128,128]{1,0:T(8,128)(2,1)} %bitcast.5, s32[8]{0:T(128)} %bitcast.7), custom_call_target="tpu_custom_call" | custom-call | tf_op jit(solution)/shard_map/exchange/pallas_call | solution.py:696
  42.3 0.7 %finish.1 = (f32[1,1,64,128]{3,2,1,0:T(8,128)}, f32[1,1,8,64,128]{4,3,2,1,0:T(8,128)}, f32[1,1,64,128]{3,2,1,0:T(8,128)}) custom-call(f32[10,64,128]{2,1,0:T(8,128)S(1)} %exchange.1.sums_ref), custom_call_target="tpu_custom_call" | custom-call | tf_op jit(solution)/shard_map/finish/pallas_call | solution.py:739

commit v5 on v4

--- a/solution.py
+++ b/solution.py
@@ -11,7 +11,7 @@
 OWN, VERT, SIDE, SIDEV = range(4)
 ROLES = ((0, 0), (0, 1), (1, 0), (1, 1))
 BLOCK = 16
-CUTS = (0, 1, 2, 4, 8)
+CUTS = (0, 2, 4, 8)
 PIECES = len(CUTS) - 1
 LEAD = 3
 WIRE = jnp.bfloat16
@@ -70,14 +70,11 @@
     load_orb = pltpu.make_async_copy(orb_hbm, orb_ref, small_sem.at[0])
     load_dens = pltpu.make_async_copy(dens_hbm, dens_ref, small_sem.at[1])
     load_mask = pltpu.make_async_copy(mask_hbm, mask_ref, small_sem.at[2])
-    load_orb.start()
-    load(0, 0).start()
-
     barrier = pltpu.get_barrier_semaphore()
     pl.semaphore_signal(barrier, inc=1, device_id=partner, device_id_type=MESH)
     expected = 1
-    for dr, row_there in ((-1, above), (0, None), (1, below)):
-        for dc, col_there in ((-1, left), (0, None), (1, right)):
+    for dc, col_there in ((0, None), (-1, left), (1, right)):
+        for dr, row_there in ((-1, above), (1, below), (0, None)):
             if dr == 0 and dc == 0:
                 continue
             there = both(
@@ -91,6 +88,9 @@
                 pl.semaphore_signal(
                     barrier, inc=1, device_id={"row": r + dr, "col": c + dc}, device_id_type=MESH
                 )
+
+    load_orb.start()
+    load(0, 0).start()
 
     def side_of(h):
         return {"col": c + 1 - 2 * h}
@@ -465,13 +465,12 @@
             gram_span(1, 0, 0, quarter)
         if i >= 2 and work:
             do(work.pop(0))
-        if (h, n) == (0, numbers[0] - 1):
-            for part in range(1, parts):
-                gram_span(0, part, 0, quarter)
     for n, o in tail:
         pass_tail(n, o)
     for items in work:
         do(items)
+    for part in range(1, parts):
+        gram_span(0, part, 0, quarter)
     products_span(0, 2, numbers[0])
 
     def swap_acc(v, h):

time: 43.2 us -> 43.1 us (level)
  no operation moved by 1% of the time
where the time goes in v5:
time: 43.1 us; the launch traced here: 42.8 us
  Pallas kernels  42.2 us (98%)
  between operations  0.64 us (1%)
    pallas_call x1, Pallas kernels, local_step(): pl.pallas_call(functools.partial(exchange_kernel, rows, cols, scales), ou...  41.5 us

profile of v5, /device:TPU:1, one launch (start us, length us, event | category | flops | bytes accessed | tf_op | source)
XLA Modules:
  0.0 42.8 jit_solution(14730000176804510426)
XLA Ops:
  0.6 41.5 %exchange.1.sums_ref = f32[10,64,128]{2,1,0:T(8,128)S(1)} custom-call(bf16[256,16384]{1,0:T(8,128)(2,1)} %bitcast.4, bf16[40,128]{1,0:T(8,128)(2,1)} %bitcast.6, bf16[128,128]{1,0:T(8,128)(2,1)} %bitcast.5, s32[8]{0:T(128)} %bitcast.7), custom_call_target="tpu_custom_call" | custom-call | tf_op jit(solution)/shard_map/exchange/pallas_call | solution.py:695
  42.1 0.7 %finish.1 = (f32[1,1,64,128]{3,2,1,0:T(8,128)}, f32[1,1,8,64,128]{4,3,2,1,0:T(8,128)}, f32[1,1,64,128]{3,2,1,0:T(8,128)}) custom-call(f32[10,64,128]{2,1,0:T(8,128)S(1)} %exchange.1.sums_ref), custom_call_target="tpu_custom_call" | custom-call | tf_op jit(solution)/shard_map/finish/pallas_call | solution.py:738
